TPU v7x, 256 devices: a whole 4x4x8 slice. The times are simulated.
256 devices in a mesh: row: 16 (over x, z_hi), col: 16 (over y, z_lo, core).
Axes of the slice: x: 4, y: 4, z: 8 (z_hi: 4, z_lo: 2; z = z_hi * 2 + z_lo), core: 2. Of those that a mesh axis runs over, the one named last changes fastest.
Arguments:
- amplitudes: bfloat16 [1280, 32768], P('row', 'col'), may hold values from -6 to 6
- integrals: bfloat16 [32768, 16384], P('col', 'row'), may hold values from -0.046875 to 0.046875
Outputs:
- ladder: bfloat16 [16384, 1280], P(('row', 'col'))
All inputs are finite; a program needn't handle non-finite values.
Results may differ from a plain program's by a relative error of at most 0.001.
Values may be sent and summed in bfloat16 or wider, within the bound.
No kernel may reach another device: no remote copies, remote signals or barrier semaphores. Data moves between devices by JAX's collectives and lax.ppermute only.
A program may use at most 64 MiB of HBM per device.

v0:
```python
import jax
import jax.numpy as jnp
from jax import lax
from jax.sharding import PartitionSpec as P


def local(amplitudes, integrals):
    partial_value = jnp.dot(
        lax.all_gather(amplitudes, "row", axis=0, tiled=True),
        integrals,
        preferred_element_type=jnp.float32,
    )
    summed = lax.psum_scatter(partial_value, "col", scatter_dimension=0, tiled=True)
    turned = summed.astype(jnp.bfloat16).T
    return lax.all_to_all(turned, "col", split_axis=0, concat_axis=1, tiled=True)


def solution(mesh):
    placed = (P("row", "col"), P("col", "row"))
    return jax.shard_map(
        local, mesh=mesh, in_specs=placed, out_specs=P(("row", "col"), None), check_vma=False
    )
```

profile of v0, /device:TPU:1, one launch (start us, length us, event | category | flops | bytes accessed | tf_op | source)
XLA Modules:
  0.0 205.7 jit_solution(17190738923694836563)
XLA Ops:
  6.5 0.0 all-gather.2.cloned.1.call-start
  6.5 0.7 all-gather.2.cloned.1.call-update
  7.3 0.0 reduce-scatter.2.cloned.1.call-start
  7.3 94.3 %all-gather.2.cloned.1.call-done = bf16[1280,2048]{1,0:T(8,128)(2,1)} async-done(((bf16[80,2048]{1,0:T(8,128)(2,1)}), bf16[1280,2048]{1,0:T(8,128)(2,1)}) %all-gather.2.cloned.1.call-update) | async-done | bytes 5242896 | tf_op jit(solution)/shard_map/all_gather | solution.py:9
  101.6 10.2 %fusion = f32[1280,1024]{1,0:T(8,128)} fusion(bf16[1280,2048]{1,0:T(8,128)(2,1)} %all-gather.2.cloned.1.call-done, bf16[2048,1024]{1,0:T(8,128)(2,1)} %param.3), kind=kOutput, calls=%fused_computation.1 | convolution fusion | flops 5368709120 | bytes 14680064 | tf_op jit(solution)/shard_map/dot_general | solution.py:8
  111.9 0.0 reduce-scatter.2.cloned.1.call-update
  111.9 71.5 %reduce-scatter.2.cloned.1.call-done = f32[80,1024]{1,0:T(8,128)} async-done(((f32[1280,1024]{1,0:T(8,128)}), f32[80,1024]{1,0:T(8,128)}) %reduce-scatter.2.cloned.1.call-update) | async-done | bytes 327696 | tf_op jit(solution)/shard_map/reduce_scatter | solution.py:13
  183.5 1.0 convert_bitcast_fusion
  184.4 0.2 copy.7
  184.6 13.1 %all_to_all.19 = bf16[16,64,80]{2,1,0:T(8,128)(2,1)S(1)} all-to-all(bf16[16,64,80]{2,1,0:T(8,128)(2,1)S(1)} %bitcast.7), channel_id=1, replica_groups=mesh['row'=16,'col'=16] {'col'}, dimensions={0} | all-to-all | bytes 327680 | tf_op jit(solution)/shard_map/all_to_all | solution.py:15
  197.8 0.2 copy.6
  197.9 0.9 all_to_all.17
Async XLA Ops:
  6.5 95.1 %all-gather.2.cloned.1.call-start = ((), (), s32[]{:S(2)}) async-start(), calls=%async_computation.2 | async-start | bytes 5570560 | tf_op jit(solution)/shard_map/all_gather | solution.py:9
  7.3 176.2 %reduce-scatter.2.cloned.1.call-start = ((), (), s32[]{:S(2)}) async-start(), calls=%async_computation.3 | async-start | bytes 5570560 | tf_op jit(solution)/shard_map/reduce_scatter | solution.py:13
Sparse Core Ops, SparseCore 0:
  9.8 91.7 all-gather.1
  112.0 71.3 reduce-scatter.1
where the time goes:
time: 206 us
  waiting for transfers between devices  167 us (81%)
  between operations  13.4 us (7%)
  blocking collectives  13.1 us (6%)
  matrix products  10.2 us (5%)
    all_gather x1, waiting for transfers between devices, local(): lax.all_gather(amplitudes, 'row', axis=0, tiled=True)  94.3 us
    reduce_scatter x1, waiting for transfers between devices, local(): lax.psum_scatter(partial_value, 'col', scatter_dimension=0, tiled=True)  71.5 us
    all_to_all x1, blocking collectives, local(): lax.all_to_all(turned, 'col', split_axis=0, concat_axis=1, tiled=True)  13.1 us
    dot_general x1, matrix products, local(): jnp.dot(lax.all_gather(amplitudes, 'row', axis=0, tiled=True), integrals,...  10.2 us
  transfers between devices with their start and end apart: 2, of which 2 were waited for; matrix products, arithmetic and copies ran while one was open for 0% of the time, Pallas kernels for 0%

commit v1 on v0

--- a/solution.py
+++ b/solution.py
@@ -4,11 +4,15 @@
 from jax.sharding import PartitionSpec as P
 
 
+def series_recast(body, group_axis):
+    u1 = lax.axis_size(group_axis)
+    res = lax.all_to_all(jnp.stack(u1 * [body], 0), group_axis, split_axis=0, concat_axis=0)
+    return jnp.concatenate(res, 0)
+
+
 def local(amplitudes, integrals):
     partial_value = jnp.dot(
-        lax.all_gather(amplitudes, "row", axis=0, tiled=True),
-        integrals,
-        preferred_element_type=jnp.float32,
+        series_recast(amplitudes, "row"), integrals, preferred_element_type=jnp.float32
     )
     summed = lax.psum_scatter(partial_value, "col", scatter_dimension=0, tiled=True)
     turned = summed.astype(jnp.bfloat16).T

time: 206 us -> 239 us (1.16)
  blocking collectives: 13.1 us -> 141 us
  waiting for transfers between devices: 167 us -> 72.4 us
  matrix products: 10.2 us -> 7.35 us
    all_to_all x0 -> x1, blocking collectives: none -> 128 us  [series_recast(): lax.all_to_all(jnp.stack(u1 * [body], 0), group_axis, split_axis=0, conca...]
    all_gather x1 -> x0, waiting for transfers between devices: 94.3 us -> none  [local(): lax.all_gather(amplitudes, 'row', axis=0, tiled=True)]
    dot_general x1, matrix products: 10.2 us -> 7.35 us  [local(): jnp.dot(series_recast(amplitudes, 'row'), integrals, preferred_element_ty...]
  transfers between devices with their start and end apart: 2 -> 1, of which waited for: 2 -> 1; matrix products, arithmetic and copies ran while one was open for 0% -> 0% of each run, Pallas kernels for 0% -> 0%
where the time goes in v1:
time: 239 us; the launch traced here: 238 us
  blocking collectives  141 us (59%)
  waiting for transfers between devices  72.4 us (30%)
  between operations  13.4 us (6%)
  matrix products  7.35 us (3%)
  local copies, waits for them, and re-layouts  2.9 us (1%)
    all_to_all x1, blocking collectives, series_recast(): lax.all_to_all(jnp.stack(u1 * [body], 0), group_axis, split_axis=0, conca...  128 us
    reduce_scatter x1, waiting for transfers between devices, local(): lax.psum_scatter(partial_value, 'col', scatter_dimension=0, tiled=True)  72.4 us
    all_to_all x1, blocking collectives, local(): lax.all_to_all(turned, 'col', split_axis=0, concat_axis=1, tiled=True)  13.1 us
    dot_general x1, matrix products, local(): jnp.dot(series_recast(amplitudes, 'row'), integrals, preferred_element_ty...  7.35 us
  transfers between devices with their start and end apart: 1, of which 1 were waited for; matrix products, arithmetic and copies ran while one was open for 0% of the time, Pallas kernels for 0%

profile of v1, /device:TPU:1, one launch (start us, length us, event | category | flops | bytes accessed | tf_op | source)
XLA Modules:
  0.0 238.4 jit_solution(12850287902368599128)
XLA Ops:
  6.5 0.0 reduce-scatter.2.cloned.1.call-start
  6.5 1.6 stack.2
  8.2 0.0 copy-start
  8.2 128.1 %all_to_all.24 = bf16[16,80,2048]{2,1,0:T(8,128)(2,1)S(1)} all-to-all(bf16[16,80,2048]{2,1,0:T(8,128)(2,1)S(1)} %stack.2), channel_id=1, replica_groups=mesh['row'=16,'col'=16] {'row'}, dimensions={0} | all-to-all | bytes 10485760 | tf_op jit(solution)/shard_map/all_to_all | solution.py:9
  136.3 0.0 copy-done
  136.3 7.3 %fusion = f32[1280,1024]{1,0:T(8,128)} fusion(bf16[1280,2048]{1,0:T(8,128)(2,1)S(1)} %bitcast.7, bf16[2048,1024]{1,0:T(8,128)(2,1)S(1)} %copy-done), kind=kOutput, calls=%fused_computation.1 | convolution fusion | flops 5368709120 | bytes 14680064 | tf_op jit(solution)/shard_map/dot_general | solution.py:14
  143.7 0.0 reduce-scatter.2.cloned.1.call-update
  143.7 72.4 %reduce-scatter.2.cloned.1.call-done = f32[80,1024]{1,0:T(8,128)} async-done(((f32[1280,1024]{1,0:T(8,128)}), f32[80,1024]{1,0:T(8,128)}) %reduce-scatter.2.cloned.1.call-update) | async-done | bytes 327696 | tf_op jit(solution)/shard_map/reduce_scatter | solution.py:17
  216.1 1.0 convert_bitcast_fusion
  217.1 0.2 copy.7
  217.3 13.1 %all_to_all.25 = bf16[16,64,80]{2,1,0:T(8,128)(2,1)S(1)} all-to-all(bf16[16,64,80]{2,1,0:T(8,128)(2,1)S(1)} %bitcast.9), channel_id=1, replica_groups=mesh['row'=16,'col'=16] {'col'}, dimensions={0} | all-to-all | bytes 327680 | tf_op jit(solution)/shard_map/all_to_all | solution.py:19
  230.4 0.2 copy.6
  230.6 0.9 all_to_all.21
Async XLA Ops:
  6.5 209.6 %reduce-scatter.2.cloned.1.call-start = ((), (), s32[]{:S(2)}) async-start(), calls=%async_computation.3 | async-start | bytes 5570560 | tf_op jit(solution)/shard_map/reduce_scatter | solution.py:17
  8.2 128.2 %copy-start = (bf16[2048,1024]{1,0:T(8,128)(2,1)S(1)}, bf16[2048,1024]{1,0:T(8,128)(2,1)}, u32[]{:S(2)}) copy-start(bf16[2048,1024]{1,0:T(8,128)(2,1)} %param.3) | copy-start | bytes 12582916
Sparse Core Ops, SparseCore 0:
  143.8 72.2 reduce-scatter.1
